TPU v7x, 512 devices: a whole 4x8x8 slice. The times are simulated.
512 devices in a mesh: row: 8 (over z), col: 8 (over x, y_hi), pair: 8 (over y_lo, core).
Axes of the slice: x: 4, y: 8 (y_hi: 2, y_lo: 4; y = y_hi * 4 + y_lo), z: 8, core: 2. Of those that a mesh axis runs over, the one named last changes fastest.
Arguments:
- pair_slab: bfloat16 [3072, 16384], P('pair', 'row'), may hold values from -0.4375 to 0.4375
- pair_weights: float32 [3072], P('pair'), may hold values from 0.2 to 2
Outputs:
- polarizability: float32 [16384, 16384], P('row', ('col', 'pair'))
All inputs are finite; a program needn't handle non-finite values.
Results may differ from a plain program's by a relative error of at most 0.0085.
Values may be sent and summed in bfloat16 or wider, within the bound.
A program may use at most 64 MiB of HBM per device.

v0:
```python
import jax
import jax.numpy as jnp
from jax import lax
from jax.sharding import PartitionSpec as P


def from_root(block, axis, owner):
    block = jnp.where(lax.axis_index(axis) == owner, block, jnp.zeros_like(block))
    return lax.psum(block, axis)


def contract_pairs(left, right):
    return lax.dot_general(
        left, right, (((0,), (0,)), ((), ())), preferred_element_type=jnp.float32
    )


def on_device(pair_slab, pair_weights):
    col_index = lax.axis_index("col")
    column_block = from_root(pair_slab, "row", col_index)
    own_columns = lax.all_to_all(column_block, "pair", split_axis=1, concat_axis=0, tiled=True)
    rows_piece = lax.all_gather(pair_slab, "pair", axis=0, tiled=True)
    weight_piece = lax.all_gather(
        pair_weights.astype(jnp.bfloat16), "pair", axis=0, tiled=True
    ).astype(jnp.float32)
    weighted = (weight_piece[:, None] * rows_piece.astype(jnp.float32)).astype(jnp.bfloat16)
    return contract_pairs(weighted, own_columns)


def solution(mesh):
    placed = (P("pair", "row"), P("pair"))
    return jax.shard_map(
        on_device, mesh=mesh, in_specs=placed, out_specs=P("row", ("col", "pair")), check_vma=False
    )
```

profile of v0, /device:TPU:9, one launch (start us, length us, event | category | flops | bytes accessed | tf_op | source)
XLA Modules:
  0.0 204.4 jit_solution(2897368251389527808)
XLA Ops:
  7.4 0.0 all-reduce.2.cloned.1.call-start
  7.4 1.9 copy.5
  9.3 1.3 broadcast_select_fusion
  10.5 0.0 all-reduce.2.cloned.1.call-update
  10.6 0.0 all-gather.3.cloned.1.call-start
  10.6 0.5 all-gather.3.cloned.1.call-update
  11.2 0.0 copy-start
  11.2 85.3 %all-reduce.2.cloned.1.call-done = bf16[384,8,256]{0,2,1:T(8,128)(2,1)} async-done(((bf16[384,8,256]{0,2,1:T(8,128)(2,1)}), bf16[384,8,256]{0,2,1:T(8,128)(2,1)}) %all-reduce.2.cloned.1.call-update) | async-done | bytes 1572880 | tf_op jit(solution)/shard_map/psum | solution.py:9
  96.5 9.2 %all-to-all-start = ((bf16[384,8,256]{0,2,1:T(8,128)(2,1)}), bf16[384,8,256]{0,2,1:T(8,128)(2,1)S(1)}, u32[]{:S(2)}, u32[]{:S(2)}) async-start(bf16[384,8,256]{0,2,1:T(8,128)(2,1)} %all-reduce.2.cloned.1.call-done), calls=%async_computation | async-start | bytes 3145728 | tf_op jit(solution)/shard_map/all_to_all | solution.py:21
  105.7 0.0 copy-done
  105.7 65.9 %all-gather = bf16[8,1,384]{2,1,0:T(2,128)(2,1)S(1)} all-gather(bf16[1,1,384]{2,1,0:T(2,128)(2,1)S(1)} %reshape.4), channel_id=1, replica_groups=mesh['row'=8,'col'=8,'pair'=8] {'pair'}, dimensions={0}, use_global_device_ids=true | all-gather | bytes 6912 | tf_op jit(solution)/shard_map/all_gather | solution.py:23
  171.6 0.0 all-to-all-done
  171.7 0.8 copy.6
  172.4 13.9 %all-gather.3.cloned.1.call-done = bf16[3072,2048]{1,0:T(8,128)(2,1)} async-done(((bf16[384,2048]{1,0:T(8,128)(2,1)}), bf16[3072,2048]{1,0:T(8,128)(2,1)}) %all-gather.3.cloned.1.call-update) | async-done | bytes 12582928 | tf_op jit(solution)/shard_map/all_gather | solution.py:22
  186.3 10.6 %fusion = f32[2048,256]{1,0:T(8,128)} fusion(bf16[3072,256]{1,0:T(8,128)(2,1)S(1)} %bitcast.7, bf16[3072,2048]{1,0:T(8,128)(2,1)} %all-gather.3.cloned.1.call-done, f32[3072]{0:T(1024)S(1)} %bitcast.8), kind=kOutput, calls=%fused_computation.1 | convolution fusion | flops 3240099840 | bytes 16265216 | tf_op jit(solution)/shard_map/dot_general | solution.py:13
  (3 shorter events, 0.0 us)
Async XLA Ops:
  7.4 89.1 %all-reduce.2.cloned.1.call-start = ((), (), s32[]{:S(2)}) async-start(), calls=%async_computation.2 | async-start | bytes 3145728 | tf_op jit(solution)/shard_map/psum | solution.py:9
  10.6 175.7 %all-gather.3.cloned.1.call-start = ((), (), s32[]{:S(2)}) async-start(), calls=%async_computation.1 | async-start | bytes 14155776 | tf_op jit(solution)/shard_map/all_gather | solution.py:22
  11.2 94.5 %copy-start = (f32[384]{0:T(512)S(1)}, f32[384]{0:T(512)}, u32[]{:S(2)}) copy-start(f32[384]{0:T(512)} %param.3) | copy-start | bytes 4612
  96.5 75.2 %all-to-all-start = ((bf16[384,8,256]{0,2,1:T(8,128)(2,1)}), bf16[384,8,256]{0,2,1:T(8,128)(2,1)S(1)}, u32[]{:S(2)}, u32[]{:S(2)}) async-start(bf16[384,8,256]{0,2,1:T(8,128)(2,1)} %all-reduce.2.cloned.1.call-done), calls=%async_computation | async-start | bytes 3145728 | tf_op jit(solution)/shard_map/all_to_all | solution.py:21
Sparse Core Ops, SparseCore 0:
  10.7 85.7 all-reduce.1
Sparse Core Ops, SparseCore 1:
  13.1 173.1 all-gather.2
where the time goes:
time: 205 us; the launch traced here: 204 us
  waiting for transfers between devices  99.8 us (49%)
  blocking collectives  65.9 us (32%)
  between operations  14.9 us (7%)
  matrix products  10.6 us (5%)
  starting transfers between devices  9.26 us (5%)
  local copies, waits for them, and re-layouts  2.63 us (1%)
    psum x1, waiting for transfers between devices, from_root(): return lax.psum(block, axis)  85.3 us
    all_gather x1, blocking collectives, on_device(): lax.all_gather(pair_weights.astype(jnp.bfloat16), 'pair', axis=0, tiled=T...  65.9 us
    all_gather x1, waiting for transfers between devices, on_device(): rows_piece = lax.all_gather(pair_slab, 'pair', axis=0, tiled=True)  13.9 us
    dot_general x1, matrix products, contract_pairs(): lax.dot_general(left, right, (((0,), (0,)), ((), ())), preferred_element_...  10.6 us
    all_to_all x1, starting transfers between devices, on_device(): lax.all_to_all(column_block, 'pair', split_axis=1, concat_axis=0, tiled=T...  9.21 us
  transfers between devices with their start and end apart: 3, of which 2 were waited for; matrix products, arithmetic and copies ran while one was open for 0% of the time, Pallas kernels for 0%

commit v1 on v0

--- a/solution.py
+++ b/solution.py
@@ -2,6 +2,13 @@
 import jax.numpy as jnp
 from jax import lax
 from jax.sharding import PartitionSpec as P
+
+
+def exchange_gather(block, mesh_axis, along):
+    count = lax.axis_size(mesh_axis)
+    blocks = jnp.stack([block for _ in range(count)])
+    blocks = lax.all_to_all(blocks, mesh_axis, split_axis=0, concat_axis=0)
+    return jnp.concatenate(blocks, axis=along)
 
 
 def from_root(block, axis, owner):
@@ -20,9 +27,7 @@
     column_block = from_root(pair_slab, "row", col_index)
     own_columns = lax.all_to_all(column_block, "pair", split_axis=1, concat_axis=0, tiled=True)
     rows_piece = lax.all_gather(pair_slab, "pair", axis=0, tiled=True)
-    weight_piece = lax.all_gather(
-        pair_weights.astype(jnp.bfloat16), "pair", axis=0, tiled=True
-    ).astype(jnp.float32)
+    weight_piece = exchange_gather(pair_weights.astype(jnp.bfloat16), "pair", 0).astype(jnp.float32)
     weighted = (weight_piece[:, None] * rows_piece.astype(jnp.float32)).astype(jnp.bfloat16)
     return contract_pairs(weighted, own_columns)
 

time: 205 us -> 205 us (level)
  blocking collectives: 65.9 us -> 12.3 us
  waiting for transfers between devices: 99.8 us -> 152 us
    all_gather x1 -> x0, blocking collectives: 65.9 us -> none  [on_device(): lax.all_gather(pair_weights.astype(jnp.bfloat16), 'pair', axis=0, tiled=T...]
    all_to_all x1, waiting for transfers between devices: 0.01 us -> 59 us  [on_device(): lax.all_to_all(column_block, 'pair', split_axis=1, concat_axis=0, tiled=T...]
    psum x1, waiting for transfers between devices: 85.3 us -> 71.7 us  [from_root(): return lax.psum(block, axis)]
    all_to_all x0 -> x1, blocking collectives: none -> 12.3 us  [exchange_gather(): blocks = lax.all_to_all(blocks, mesh_axis, split_axis=0, concat_axis=0)]
    all_gather x1, waiting for transfers between devices: 13.9 us -> 20.7 us  [on_device(): rows_piece = lax.all_gather(pair_slab, 'pair', axis=0, tiled=True)]
  transfers between devices with their start and end apart: 3 -> 3, of which waited for: 2 -> 3; matrix products, arithmetic and copies ran while one was open for 0% -> 1% of each run, Pallas kernels for 0% -> 0%
where the time goes in v1:
time: 205 us; the launch traced here: 204 us
  waiting for transfers between devices  152 us (74%)
  between operations  14.9 us (7%)
  blocking collectives  12.3 us (6%)
  matrix products  10.6 us (5%)
  starting transfers between devices  9.26 us (5%)
  local copies, waits for them, and re-layouts  3.41 us (2%)
    psum x1, waiting for transfers between devices, from_root(): return lax.psum(block, axis)  71.7 us
    all_to_all x1, waiting for transfers between devices, on_device(): lax.all_to_all(column_block, 'pair', split_axis=1, concat_axis=0, tiled=T...  59 us
    all_gather x1, waiting for transfers between devices, on_device(): rows_piece = lax.all_gather(pair_slab, 'pair', axis=0, tiled=True)  20.7 us
    all_to_all x1, blocking collectives, exchange_gather(): blocks = lax.all_to_all(blocks, mesh_axis, split_axis=0, concat_axis=0)  12.3 us
    dot_general x1, matrix products, contract_pairs(): lax.dot_general(left, right, (((0,), (0,)), ((), ())), preferred_element_...  10.6 us
    all_to_all x1, starting transfers between devices, on_device(): lax.all_to_all(column_block, 'pair', split_axis=1, concat_axis=0, tiled=T...  9.21 us
  transfers between devices with their start and end apart: 3, of which 3 were waited for; matrix products, arithmetic and copies ran while one was open for 1% of the time, Pallas kernels for 0%

profile of v1, /device:TPU:9, one launch (start us, length us, event | category | flops | bytes accessed | tf_op | source)
XLA Modules:
  0.0 204.3 jit_solution(17775802150731279791)
XLA Ops:
  7.4 0.0 all-reduce.2.cloned.1.call-start
  7.4 1.9 copy.3
  9.3 1.3 broadcast_select_fusion
  10.5 0.0 copy-start
  10.6 0.0 all-reduce.2.cloned.1.call-update
  10.6 0.0 all-gather.2.cloned.1.call-start
  10.6 0.5 all-gather.2.cloned.1.call-update
  11.2 0.1 copy-done
  11.2 0.5 broadcast.4
  11.8 0.7 reduce
  12.5 0.1 reshape.20
  12.5 12.3 %all_to_all.25 = bf16[8,2,192]{2,1,0:T(2,128)(2,1)S(1)} all-to-all(bf16[8,2,192]{2,1,0:T(2,128)(2,1)S(1)} %reshape.20), channel_id=1, replica_groups=mesh['row'=8,'col'=8,'pair'=8] {'pair'}, dimensions={0} | all-to-all | bytes 12288 | tf_op jit(solution)/shard_map/all_to_all | solution.py:10
  24.8 71.7 %all-reduce.2.cloned.1.call-done = bf16[384,8,256]{0,2,1:T(8,128)(2,1)} async-done(((bf16[384,8,256]{0,2,1:T(8,128)(2,1)}), bf16[384,8,256]{0,2,1:T(8,128)(2,1)}) %all-reduce.2.cloned.1.call-update) | async-done | bytes 1572880 | tf_op jit(solution)/shard_map/psum | solution.py:16
  96.5 9.2 %all-to-all-start.1 = ((bf16[384,8,256]{0,2,1:T(8,128)(2,1)}), bf16[384,8,256]{0,2,1:T(8,128)(2,1)S(1)}, u32[]{:S(2)}, u32[]{:S(2)}) async-start(bf16[384,8,256]{0,2,1:T(8,128)(2,1)} %all-reduce.2.cloned.1.call-done), calls=%async_computation.1 | async-start | bytes 3145728 | tf_op jit(solution)/shard_map/all_to_all | solution.py:28
  105.7 0.1 reshape.21
  105.8 59.0 %all-to-all-done.1 = bf16[384,8,256]{0,2,1:T(8,128)(2,1)S(1)} async-done(((bf16[384,8,256]{0,2,1:T(8,128)(2,1)}), bf16[384,8,256]{0,2,1:T(8,128)(2,1)S(1)}, u32[]{:S(2)}, u32[]{:S(2)}) %all-to-all-start.1) | async-done | bytes 1572896 | tf_op jit(solution)/shard_map/all_to_all | solution.py:28
  164.8 0.7 copy.4
  165.5 20.7 %all-gather.2.cloned.1.call-done = bf16[3072,2048]{1,0:T(8,128)(2,1)} async-done(((bf16[384,2048]{1,0:T(8,128)(2,1)}), bf16[3072,2048]{1,0:T(8,128)(2,1)}) %all-gather.2.cloned.1.call-update) | async-done | bytes 12582928 | tf_op jit(solution)/shard_map/all_gather | solution.py:29
  186.2 10.6 %fusion = f32[2048,256]{1,0:T(8,128)} fusion(bf16[3072,256]{1,0:T(8,128)(2,1)S(1)} %bitcast.7, bf16[3072,2048]{1,0:T(8,128)(2,1)} %all-gather.2.cloned.1.call-done, f32[3072]{0:T(1024)S(1)} %bitcast.8), kind=kOutput, calls=%fused_computation.1 | convolution fusion | flops 3240099840 | bytes 16265216 | tf_op jit(solution)/shard_map/dot_general | solution.py:20
  (3 shorter events, 0.0 us)
Async XLA Ops:
  7.4 89.1 %all-reduce.2.cloned.1.call-start = ((), (), s32[]{:S(2)}) async-start(), calls=%async_computation.3 | async-start | bytes 3145728 | tf_op jit(solution)/shard_map/psum | solution.py:16
  10.5 0.7 copy-start
  10.6 175.6 %all-gather.2.cloned.1.call-start = ((), (), s32[]{:S(2)}) async-start(), calls=%async_computation.2 | async-start | bytes 14155776 | tf_op jit(solution)/shard_map/all_gather | solution.py:29
  96.5 68.3 %all-to-all-start.1 = ((bf16[384,8,256]{0,2,1:T(8,128)(2,1)}), bf16[384,8,256]{0,2,1:T(8,128)(2,1)S(1)}, u32[]{:S(2)}, u32[]{:S(2)}) async-start(bf16[384,8,256]{0,2,1:T(8,128)(2,1)} %all-reduce.2.cloned.1.call-done), calls=%async_computation.1 | async-start | bytes 3145728 | tf_op jit(solution)/shard_map/all_to_all | solution.py:28
Sparse Core Ops, SparseCore 0:
  10.7 85.7 all-reduce.1
Sparse Core Ops, SparseCore 1:
  13.1 173.0 all-gather.1
